TPU v7x, 256 devices: a whole 4x4x8 slice. The times are simulated.
256 devices in a mesh: pair: 8 (over y, z_lo), virt: 32 (over x, z_hi, core).
Axes of the slice: x: 4, y: 4, z: 8 (z_hi: 4, z_lo: 2; z = z_hi * 2 + z_lo), core: 2. Of those that a mesh axis runs over, the one named last changes fastest.
Arguments:
- amplitudes: bfloat16 [8192, 131072], P('pair', 'virt'), may hold values from -6 to 6
- integrals: bfloat16 [131072, 1024], P('virt', 'pair'), may hold values from -0.015625 to 0.015625
- occ_pairs: int32 [8192, 2], P(('pair', 'virt')), may hold values from 0 to 95, as said below
- partners: int32 [8192], P(('pair', 'virt')), may hold values from 0 to 8191, as said below
- virt_list: int32 [32], replicated, may hold values from 0 to 511
- eps_occ: float32 [96], replicated, may hold values from -2 to -0.5
- eps_virt: float32 [512], replicated, may hold values from 0.2 to 3
Outputs:
- update: float32 [8192, 1024], P(('pair', 'virt'))
Inputs may be any that keep to these rules, and one draw needn't show every extreme that they name: Row r holds the pair (i, j) with i != j; row partners[r] holds (j, i), partners[partners[r]] = r, and partners[r] lies in the same index of pair and in the index of virt 32 / 2 away under the placement of the output rows. `occ_pairs`: the two orbitals of a row differ.
All inputs are finite; a program needn't handle non-finite values.
Results may differ from a plain program's by a relative error of at most 0.0003.
Values may be sent and summed in bfloat16 or wider, within the bound.
A program may use at most 192 MiB of HBM per device.

v0:
```python
import jax
import jax.numpy as jnp
from jax import lax
from jax.sharding import PartitionSpec as P


def passed_along(value, axis, steps):
    count = lax.axis_size(axis)
    pairs = [(source, (source + steps) % count) for source in range(count)]
    return lax.ppermute(value, axis, pairs)


def transpose_block(values, width):
    count = values.shape[0]
    return values.reshape(count, width, width).transpose(0, 2, 1).reshape(count, width * width)


def add_transposed(mine, partners, width):
    other = passed_along(mine, "virt", lax.axis_size("virt") // 2)
    local_rows = partners % mine.shape[0]
    flipped = jnp.take(other, local_rows, axis=0)
    return mine + transpose_block(flipped, width)


def columns_product(amplitudes, integrals):
    return jnp.dot(
        amplitudes,
        lax.all_gather(integrals, "pair", axis=1, tiled=True),
        preferred_element_type=jnp.float32,
    )


def per_device(amplitudes, integrals, occ_pairs, partners, virt_list, eps_occ, eps_virt):
    width = virt_list.shape[0]
    partial_value = columns_product(amplitudes, integrals)
    mine = lax.psum_scatter(partial_value, "virt", scatter_dimension=0, tiled=True)
    total = add_transposed(mine, partners, width)
    occ_ids = jnp.arange(eps_occ.shape[0], dtype=jnp.int32)
    occ_match = occ_pairs[:, :, None] == occ_ids[None, None, :]
    occ_sum = jnp.sum(jnp.where(occ_match, eps_occ[None, None, :], 0.0), axis=(1, 2))
    virt_ids = jnp.arange(eps_virt.shape[0], dtype=jnp.int32)
    virt_match = virt_list[:, None] == virt_ids[None, :]
    virt_energy = jnp.sum(jnp.where(virt_match, eps_virt[None, :], 0.0), axis=1)
    virt_sum = (virt_energy[:, None] + virt_energy[None, :]).reshape(-1)
    denominator = virt_sum[None, :] - occ_sum[:, None]
    return total / denominator


def solution(mesh):
    placed = (
        P("pair", "virt"),
        P("virt", "pair"),
        P(("pair", "virt"), None),
        P(("pair", "virt")),
        P(),
        P(),
        P(),
    )
    return jax.shard_map(
        per_device, mesh=mesh, in_specs=placed, out_specs=P(("pair", "virt"), None), check_vma=False
    )
```

profile of v0, /device:TPU:8, one launch (start us, length us, event | category | flops | bytes accessed | tf_op | source)
XLA Modules:
  0.0 315.1 jit_solution(4801339401054413882)
XLA Ops:
  6.5 0.0 all-gather.2.cloned.1.call-start
  6.5 0.7 all-gather.2.cloned.1.call-update
  7.3 0.0 copy-start
  7.3 0.0 copy-start.2
  7.3 0.0 copy-start.4
  7.3 0.0 copy-start.1
  7.3 0.0 copy-start.3
  7.3 0.0 reduce-scatter.2.cloned.1.call-start
  7.4 175.3 %all-gather.2.cloned.1.call-done = bf16[4096,1024]{1,0:T(8,128)(2,1)} async-done(((bf16[4096,128]{1,0:T(8,128)(2,1)}), bf16[4096,1024]{1,0:T(8,128)(2,1)}) %all-gather.2.cloned.1.call-update) | async-done | bytes 8388624 | tf_op jit(solution)/shard_map/all_gather | solution.py:28
  182.6 15.0 %fusion.1 = f32[1024,1024]{1,0:T(8,128)} fusion(bf16[1024,4096]{1,0:T(8,128)(2,1)} %param.7, bf16[4096,1024]{1,0:T(8,128)(2,1)} %all-gather.2.cloned.1.call-done), kind=kOutput, calls=%fused_computation.15 | convolution fusion | flops 8589934592 | bytes 20971520 | tf_op jit(solution)/shard_map/dot_general | solution.py:26
  197.7 0.0 reduce-scatter.2.cloned.1.call-update
  197.7 0.0 copy-done
  197.7 0.0 copy-done.2
  197.7 0.2 select_reduce_fusion
  197.9 0.0 copy-done.4
  197.9 0.1 broadcast_add_fusion
  198.0 100.5 %reduce-scatter.2.cloned.1.call-done = f32[32,1024]{1,0:T(8,128)} async-done(((f32[1024,1024]{1,0:T(8,128)}), f32[32,1024]{1,0:T(8,128)}) %reduce-scatter.2.cloned.1.call-update) | async-done | bytes 131088 | tf_op jit(solution)/shard_map/reduce_scatter | solution.py:36
  298.5 1.6 collective-permute-start
  300.2 0.1 add.43
  300.2 0.0 copy-done.1
  300.2 0.0 copy-done.3
  300.2 0.2 select_reduce_fusion.1
  300.4 4.8 %collective-permute-done = f32[32,1024]{1,0:T(8,128)S(1)} collective-permute-done((f32[32,1024]{1,0:T(8,128)}, f32[32,1024]{1,0:T(8,128)S(1)}, u32[]{:S(2)}, u32[]{:S(2)}) %collective-permute-start) | collective-permute-done | bytes 131104 | tf_op jit(solution)/shard_map/ppermute | solution.py:10
  305.2 0.6 gather_fusion
  305.8 0.2 gather.7
  306.0 0.2 copy.10
  306.2 0.1 select_bitcast_fusion
  306.3 0.2 reshape.36
  306.6 1.7 subtract_divide_fusion
  (2 shorter events, 0.0 us)
Async XLA Ops:
  6.5 176.1 %all-gather.2.cloned.1.call-start = ((), (), s32[]{:S(2)}) async-start(), calls=%async_computation.1 | async-start | bytes 9437184 | tf_op jit(solution)/shard_map/all_gather | solution.py:28
  7.3 190.4 %copy-start = (f32[512]{0:T(512)S(1)}, f32[512]{0:T(512)}, u32[]{:S(2)}) copy-start(f32[512]{0:T(512)} %param.13) | copy-start | bytes 6148
  7.3 190.4 %copy-start.2 = (s32[32]{0:T(128)S(1)}, s32[32]{0:T(128)}, u32[]{:S(2)}) copy-start(s32[32]{0:T(128)} %param.11) | copy-start | bytes 388
  7.3 190.6 %copy-start.4 = (s32[32]{0:T(128)S(1)}, s32[32]{0:T(128)}, u32[]{:S(2)}) copy-start(s32[32]{0:T(128)} %param.10) | copy-start | bytes 388
  7.3 293.0 %copy-start.1 = (s32[32,2]{0,1:T(2,128)S(1)}, s32[32,2]{0,1:T(2,128)}, u32[]{:S(2)}) copy-start(s32[32,2]{0,1:T(2,128)} %param.9) | copy-start | bytes 772
  7.3 293.0 %copy-start.3 = (f32[96]{0:T(128)S(1)}, f32[96]{0:T(128)}, u32[]{:S(2)}) copy-start(f32[96]{0:T(128)} %param.12) | copy-start | bytes 1156
  7.3 291.2 %reduce-scatter.2.cloned.1.call-start = ((), (), s32[]{:S(2)}) async-start(), calls=%async_computation.2 | async-start | bytes 4325376 | tf_op jit(solution)/shard_map/reduce_scatter | solution.py:36
  298.5 6.7 %collective-permute-start = (f32[32,1024]{1,0:T(8,128)}, f32[32,1024]{1,0:T(8,128)S(1)}, u32[]{:S(2)}, u32[]{:S(2)}) collective-permute-start(f32[32,1024]{1,0:T(8,128)} %reduce-scatter.2.cloned.1.call-done), channel_id=1, source_target_pairs={{0,16},{1,17},{2,18},{3,19},{4,20},{5,21},{6,22},{7,23},{8,24},{9,... | collective-permute-start | bytes 393224 | tf_op jit(solution)/shard_map/ppermute | solution.py:10
Sparse Core Ops, SparseCore 0:
  9.0 173.5 all-gather.1
  197.8 100.6 reduce-scatter.1
where the time goes:
time: 315 us
  waiting for transfers between devices  281 us (89%)
  matrix products  15 us (5%)
  between operations  13.5 us (4%)
    all_gather x1, waiting for transfers between devices, columns_product(): lax.all_gather(integrals, 'pair', axis=1, tiled=True)  175 us
    reduce_scatter x1, waiting for transfers between devices, per_device(): lax.psum_scatter(partial_value, 'virt', scatter_dimension=0, tiled=True)  101 us
    dot_general x1, matrix products, columns_product(): jnp.dot(amplitudes, lax.all_gather(integrals, 'pair', axis=1, tiled=True)...  15 us
  transfers between devices with their start and end apart: 3, of which 3 were waited for; matrix products, arithmetic and copies ran while one was open for 0% of the time, Pallas kernels for 0%

commit v1 on v0

v1 whole, which is shorter than its diff:
```python
import functools

import jax
import jax.numpy as jnp
from jax import lax
from jax.experimental import pallas as pl
from jax.experimental.pallas import tpu as pltpu
from jax.sharding import PartitionSpec as P

F32 = jnp.float32
NY, NX, NH = 4, 4, 4
CHUNKS = 16
FIRST_Z = 10
GROUP = 256
MT = 256


def ladder_kernel(
    a_hbm, b_hbm, mine_ref, other_ref,
    a_v, b_v, c_v, r1_v, d_v, ra_v, rb_v, rc_v, rd_v, e_v, rz_v, m_v, o_v,
    a_sem, b_sem, ag_s, ag_r, s1_s, s1_r, sx_s, sx_r, sz_s, sz_r, so_s, so_r,
):
    nc, n1 = CHUNKS, FIRST_Z
    ch = b_v.shape[1]
    pair, virt = lax.axis_index("pair"), lax.axis_index("virt")
    y, z = pair // 2, pair % 2
    x, zh, core = virt // 8, (virt // 2) % 4, virt % 2

    def device(ny, nz, nx, nh, ncore):
        return {"pair": ny * 2 + nz, "virt": (nx * 4 + nh) * 2 + ncore}

    y_up, y_dn = (y + 1) % NY, (y + 3) % NY
    x_up, x_dn, x_far = (x + 1) % NX, (x + 3) % NX, (x + 2) % NX
    h_others = [(zh + 1) % NH, (zh + 3) % NH, (zh + 2) % NH]
    to_z = device(y, 1 - z, x, zh, core)
    to_up = device(y_up, z, x, zh, core)
    to_dn = device(y_dn, z, x, zh, core)
    to_core = device(y, z, x, zh, 1 - core)
    to_xu = device(y, z, x_up, zh, core)
    to_xd = device(y, z, x_dn, zh, core)
    to_xf = device(y, z, x_far, zh, core)
    to_h = [device(y, z, x, h, core) for h in h_others]
    partners = [to_z, to_up, to_dn, to_core, to_xu, to_xd, to_xf] + to_h

    b_copy = []
    for c in range(nc):
        cp = pltpu.make_async_copy(b_hbm.at[pl.ds(c * ch, ch)], b_v.at[z * nc + c], b_sem.at[c])
        cp.start()
        b_copy.append(cp)
    a_copy = []
    for c in range(nc):
        cp = pltpu.make_async_copy(a_hbm.at[:, pl.ds(c * ch, ch)], a_v.at[c], a_sem.at[c])
        cp.start()
        a_copy.append(cp)

    barrier = pltpu.get_barrier_semaphore()
    for dev in partners:
        pl.semaphore_signal(barrier, inc=1, device_id=dev, device_id_type=pl.DeviceIdType.MESH)
    pl.semaphore_wait(barrier, len(partners))

    def remote(src, dst, ssem, rsem, dev):
        return pltpu.make_async_remote_copy(
            src_ref=src, dst_ref=dst, send_sem=ssem, recv_sem=rsem,
            device_id=dev, device_id_type=pl.DeviceIdType.MESH,
        )

    def slot(s, rel, c):
        plane = z if rel == 0 else 1 - z
        return (s * 2 + plane) * nc + c

    def move(s_from, rel, s_to, rel_to, c, stream, dev):
        src = b_v.at[slot(s_from, rel, c)]
        dst = b_v.at[slot(s_to, rel, c)]
        remote(src, dst, ag_s.at[stream], ag_r.at[s_to * 2 + rel_to, c], dev).start()

    def send_z(s, c):
        move(s, 0, s, 1, c, 0, to_z)

    def send_up(rel, c):
        move(0, rel, 2, rel, c, 1, to_up)

    def send_dn(rel, c):
        move(0, rel, 1, rel, c, 2, to_dn)

    def relay_up(rel, c):
        move(2, rel, 3, rel, c, 1, to_up)

    def relay_dn(rel, c):
        move(1, rel, 3, rel, c, 2, to_dn)

    def arrived(s, rel, c):
        ref = b_v.at[slot(s, rel, c)]
        remote(ref, ref, ag_s.at[0], ag_r.at[s * 2 + rel, c], to_z).wait_recv()

    def multiply(slots, chunk0, count, first):
        rows = MT // 64

        def body(i, _):
            m = i % 4
            k = chunk0 + (i // 4) % count
            s = slots[0] + i // (4 * count)
            base = s * 2 * nc + k
            rhs = jnp.concatenate([b_v[base], b_v[base + nc]], axis=1)
            lhs = a_v[k, pl.ds(pl.multiple_of(m * MT, MT), MT), :]
            part = jnp.dot(lhs, rhs, preferred_element_type=F32).reshape(rows, 2, 32, GROUP)
            at = pl.ds(m * rows, rows)
            if first:
                c_v[s, at] = part
            else:
                c_v[s, at] = c_v[s, at] + part
            return 0

        lax.fori_loop(0, 4 * count * len(slots), body, 0)

    def r_core(g):
        return remote(c_v.at[g, :, 1 - core], r1_v.at[g], s1_s.at[g], s1_r.at[g], to_core)

    def r_x(g):
        return [
            remote(d_v.at[g, x_far, 0], ra_v.at[g], sx_s.at[g, 0], sx_r.at[g, 0], to_xu),
            remote(d_v.at[g, x_far, 1], rb_v.at[g], sx_s.at[g, 1], sx_r.at[g, 1], to_xd),
            remote(d_v.at[g, x_up, 1], rc_v.at[g, 1], sx_s.at[g, 2], sx_r.at[g, 2], to_xu),
            remote(d_v.at[g, x_dn, 0], rd_v.at[g, 0], sx_s.at[g, 3], sx_r.at[g, 3], to_xd),
            remote(d_v.at[g, x_up, 0], rc_v.at[g, 0], sx_s.at[g, 4], sx_r.at[g, 4], to_xu),
            remote(d_v.at[g, x_dn, 1], rd_v.at[g, 1], sx_s.at[g, 5], sx_r.at[g, 5], to_xd),
        ]

    def r_h(g):
        return [
            remote(e_v.at[g, h_others[k]], rz_v.at[g, k], sz_s.at[g, k], sz_r.at[g, k], to_h[k])
            for k in range(3)
        ]

    def r_far(g):
        return remote(m_v.at[g], o_v.at[g], so_s.at[g], so_r.at[g], to_xf)

    def stage1(g):
        r_core(g).start()

    def stage2(g):
        r_core(g).wait_recv()
        for xx in range(NX):
            rows = pl.ds(xx * NH, NH)
            total = c_v[g, rows, core] + r1_v[g, rows]
            d_v[g, xx, 0] = total[:, :, :128]
            d_v[g, xx, 1] = total[:, :, 128:]
        copies = r_x(g)
        for k in range(4):
            copies[k].start()

    def stage3(g):
        copies = r_x(g)
        copies[0].wait_recv()
        d_v[g, x_up, 0] = d_v[g, x_up, 0] + ra_v[g]
        copies[4].start()
        copies[1].wait_recv()
        d_v[g, x_dn, 1] = d_v[g, x_dn, 1] + rb_v[g]
        copies[5].start()

    def stage4(g):
        copies = r_x(g)
        for k in range(2, 6):
            copies[k].wait_recv()
        for half in range(2):
            e_v[g, :, half] = d_v[g, x, half] + rc_v[g, half] + rd_v[g, half]
        for cp in r_h(g):
            cp.start()

    def stage5(g):
        for cp in r_h(g):
            cp.wait_recv()
        m_v[g] = e_v[g, zh] + rz_v[g, 0] + rz_v[g, 1] + rz_v[g, 2]
        r_far(g).start()

    def stage6(g):
        r_far(g).wait_recv()
        owner = [y, y_up, y_dn, (y + 2) % NY][g]
        for half in range(2):
            cols = pl.ds(pl.multiple_of(owner * GROUP + half * 128, 128), 128)
            mine_ref[:, cols] = m_v[g, half]
            other_ref[:, cols] = o_v[g, half]

    stages = [stage1, stage2, stage3, stage4, stage5, stage6]

    for c in range(nc):
        b_copy[c].wait()
    for k in range(nc):
        send_z(0, k)
        late = (k + n1) % nc
        send_up(0, late)
        send_dn(0, late)
    for c in range(nc):
        a_copy[c].wait()

    for u in range(n1 // 2):
        if u < (nc - n1) // 2:
            lo, hi = n1 + 2 * u, n1 + 2 * u + 1
            for c in (lo, hi):
                arrived(1, 0, c)
                arrived(2, 0, c)
            relay_up(0, lo)
            relay_dn(0, hi)
            for c in (lo, hi):
                send_z(1, c)
                send_z(2, c)
        for c in (2 * u, 2 * u + 1):
            arrived(0, 1, c)
            send_up(1, c)
            send_dn(1, c)
        if u == 0:
            multiply([0], 0, 1, True)
            multiply([0], 1, 1, False)
        else:
            multiply([0], 2 * u, 2, False)

    for u in range(n1 // 2):
        lo, hi = 2 * u, 2 * u + 1
        for c in (lo, hi):
            arrived(1, 0, c)
            arrived(2, 0, c)
        relay_up(0, lo)
        relay_dn(0, hi)
    for c in range(n1, nc):
        arrived(0, 1, c)
    multiply([0], n1, nc - n1, False)
    stage1(0)

    for u in range(n1 // 2):
        if u < (nc - n1) // 2:
            for c in (n1 + 2 * u, n1 + 2 * u + 1):
                arrived(3, 0, c)
                send_z(3, c)
        lo, hi = 2 * u, 2 * u + 1
        for c in (lo, hi):
            arrived(1, 1, c)
            arrived(2, 1, c)
        relay_up(1, lo)
        relay_dn(1, hi)
        if u == 0:
            multiply([1, 2], 0, 1, True)
            multiply([1, 2], 1, 1, False)
        else:
            multiply([1, 2], lo, 2, False)
        stages[u + 1](0)
    for c in range(n1, nc):
        arrived(1, 1, c)
        arrived(2, 1, c)
    multiply([1, 2], n1, nc - n1, False)
    stage1(1)
    stage1(2)

    for c in range(n1, nc):
        arrived(3, 1, c)
    multiply([3], n1, 1, True)
    multiply([3], n1 + 1, nc - n1 - 1, False)
    for c in range(n1):
        arrived(3, 0, c)
        if c % 2 == 1 and c // 2 < 5:
            stages[c // 2 + 1](1)
            stages[c // 2 + 1](2)
    for c in range(n1):
        arrived(3, 1, c)
        multiply([3], c, 1, False)
    for stage in stages:
        stage(3)

    relays = (nc + n1) // 2
    for stream, count in ((0, nc + 3 * (nc - n1)), (1, nc + n1 + relays), (2, nc + n1 + relays)):
        ref = b_v.at[pl.ds(0, count)]
        remote(ref, ref, ag_s.at[stream], ag_r.at[0, 0], to_z).wait_send()
    for g in range(4):
        for cp in [r_core(g), r_far(g)] + r_x(g) + r_h(g):
            cp.wait_send()


def ladder_rows(amplitudes, integrals):
    rows, depth = amplitudes.shape
    ch = depth // CHUNKS
    vmem, dma = pltpu.VMEM, pltpu.SemaphoreType.DMA
    out = jax.ShapeDtypeStruct((32, 1024), F32)
    return pl.pallas_call(
        ladder_kernel,
        out_shape=(out, out),
        in_specs=[pl.BlockSpec(memory_space=pl.ANY)] * 2,
        out_specs=(pl.BlockSpec(memory_space=pltpu.VMEM),) * 2,
        scratch_shapes=[
            vmem((CHUNKS, rows, ch), jnp.bfloat16),
            vmem((8 * CHUNKS, ch, 128), jnp.bfloat16),
            vmem((4, 16, 2, 32, GROUP), F32),
            vmem((4, 16, 32, GROUP), F32),
            vmem((4, NX, 2, NH, 32, 128), F32),
            vmem((4, NH, 32, 128), F32),
            vmem((4, NH, 32, 128), F32),
            vmem((4, 2, NH, 32, 128), F32),
            vmem((4, 2, NH, 32, 128), F32),
            vmem((4, NH, 2, 32, 128), F32),
            vmem((4, 3, 2, 32, 128), F32),
            vmem((4, 2, 32, 128), F32),
            vmem((4, 2, 32, 128), F32),
            dma((CHUNKS,)),
            dma((CHUNKS,)),
            dma((3,)),
            dma((8, CHUNKS)),
            dma((4,)),
            dma((4,)),
            dma((4, 6)),
            dma((4, 6)),
            dma((4, 3)),
            dma((4, 3)),
            dma((4,)),
            dma((4,)),
        ],
        compiler_params=pltpu.CompilerParams(collective_id=0, has_side_effects=True, vmem_limit_bytes=48 << 20),
    )(amplitudes, integrals)


def transpose_block(values, width):
    count = values.shape[0]
    return values.reshape(count, width, width).transpose(0, 2, 1).reshape(count, width * width)


def per_device(amplitudes, integrals, occ_pairs, partners, virt_list, eps_occ, eps_virt):
    width = virt_list.shape[0]
    mine, other = ladder_rows(amplitudes, integrals)
    flipped = jnp.take(other, partners % mine.shape[0], axis=0)
    total = mine + transpose_block(flipped, width)
    occ_ids = jnp.arange(eps_occ.shape[0], dtype=jnp.int32)
    occ_match = occ_pairs[:, :, None] == occ_ids[None, None, :]
    occ_sum = jnp.sum(jnp.where(occ_match, eps_occ[None, None, :], 0.0), axis=(1, 2))
    virt_ids = jnp.arange(eps_virt.shape[0], dtype=jnp.int32)
    virt_match = virt_list[:, None] == virt_ids[None, :]
    virt_energy = jnp.sum(jnp.where(virt_match, eps_virt[None, :], 0.0), axis=1)
    virt_sum = (virt_energy[:, None] + virt_energy[None, :]).reshape(-1)
    denominator = virt_sum[None, :] - occ_sum[:, None]
    return total / denominator


def solution(mesh):
    placed = (
        P("pair", "virt"),
        P("virt", "pair"),
        P(("pair", "virt"), None),
        P(("pair", "virt")),
        P(),
        P(),
        P(),
    )
    return jax.shard_map(
        per_device, mesh=mesh, in_specs=placed, out_specs=P(("pair", "virt"), None), check_vma=False
    )
```

time: 315 us -> 133 us (0.42)
  waiting for transfers between devices: 281 us -> 0 us
  Pallas kernels: 0 us -> 127 us
  matrix products: 15 us -> 0 us
  between operations: 13.5 us -> 0.1 us
    all_gather x1 -> x0, waiting for transfers between devices: 175 us -> none  [columns_product(): lax.all_gather(integrals, 'pair', axis=1, tiled=True)]
    pallas_call x0 -> x1, Pallas kernels: none -> 127 us  [ladder_rows(): pl.pallas_call(ladder_kernel, out_shape=(out, out), in_specs=[pl.BlockSpe...]
    reduce_scatter x1 -> x0, waiting for transfers between devices: 101 us -> none  [per_device(): lax.psum_scatter(partial_value, 'virt', scatter_dimension=0, tiled=True)]
    dot_general x1 -> x0, matrix products: 15 us -> none  [columns_product(): jnp.dot(amplitudes, lax.all_gather(integrals, 'pair', axis=1, tiled=True)...]
    ppermute x1 -> x0, waiting for transfers between devices: 4.8 us -> none  [passed_along(): return lax.ppermute(value, axis, pairs)]
  transfers between devices with their start and end apart: 3 -> 0, of which waited for: 3 -> 0; matrix products, arithmetic and copies ran while one was open for 0% -> 0% of each run, Pallas kernels for 0% -> 0%
where the time goes in v1:
time: 133 us; the launch traced here: 131 us
  Pallas kernels  127 us (95%)
  local copies, waits for them, and re-layouts  2.54 us (2%)
    pallas_call x1, Pallas kernels, ladder_rows(): pl.pallas_call(ladder_kernel, out_shape=(out, out), in_specs=[pl.BlockSpe...  127 us

profile of v1, /device:TPU:8, one launch (start us, length us, event | category | flops | bytes accessed | tf_op | source)
XLA Modules:
  0.0 131.0 jit_solution(92054968617631337)
XLA Ops:
  0.0 0.0 copy-start
  0.0 1.2 copy-done
  1.2 0.0 copy-start.5
  1.2 0.0 copy-start.2
  1.2 0.0 copy-start.3
  1.2 0.0 copy-start.1
  1.2 0.0 copy-start.4
  1.2 127.0 %shard_map.73 = (f32[32,1024]{1,0:T(8,128)S(1)}, f32[32,1024]{1,0:T(8,128)S(1)}) custom-call(bf16[1024,4096]{1,0:T(8,128)(2,1)} %a_hbm.1, bf16[4096,128]{1,0:T(8,128)(2,1)S(1)} %copy-done), custom_call_target="tpu_custom_call" | custom-call | tf_op jit(solution)/shard_map/pallas_call | solution.py:281
  128.3 0.0 copy-done.5
  128.3 0.6 gather_fusion
  128.9 0.2 gather.7
  129.1 0.2 copy.10
  129.3 0.1 select_bitcast_fusion
  129.4 0.2 reshape.36
  129.7 0.0 copy-done.2
  129.7 0.0 copy-done.3
  129.7 0.2 select_reduce_fusion.1
  129.9 0.0 copy-done.1
  129.9 0.0 copy-done.4
  129.9 0.2 select_reduce_fusion
  130.1 0.1 broadcast_add_fusion
  130.1 0.1 add.41
  130.2 0.8 subtract_divide_fusion
  (2 shorter events, 0.0 us)
Async XLA Ops:
  0.0 1.2 copy-start
  1.2 127.0 %copy-start.5 = (s32[32]{0:T(128)S(1)}, s32[32]{0:T(128)}, u32[]{:S(2)}) copy-start(s32[32]{0:T(128)} %param.10) | copy-start | bytes 388
  1.2 128.4 %copy-start.2 = (s32[32,2]{0,1:T(2,128)S(1)}, s32[32,2]{0,1:T(2,128)}, u32[]{:S(2)}) copy-start(s32[32,2]{0,1:T(2,128)} %param.9) | copy-start | bytes 772
  1.2 128.4 %copy-start.3 = (f32[96]{0:T(128)S(1)}, f32[96]{0:T(128)}, u32[]{:S(2)}) copy-start(f32[96]{0:T(128)} %param.12) | copy-start | bytes 1156
  1.2 128.6 %copy-start.1 = (f32[512]{0:T(512)S(1)}, f32[512]{0:T(512)}, u32[]{:S(2)}) copy-start(f32[512]{0:T(512)} %param.13) | copy-start | bytes 6148
  1.2 128.6 %copy-start.4 = (s32[32]{0:T(128)S(1)}, s32[32]{0:T(128)}, u32[]{:S(2)}) copy-start(s32[32]{0:T(128)} %param.11) | copy-start | bytes 388

commit v2 on v1

v2 whole, which is shorter than its diff:
```python
import jax
import jax.numpy as jnp
from jax import lax
from jax.experimental import pallas as pl
from jax.experimental.pallas import tpu as pltpu
from jax.sharding import PartitionSpec as P

F32 = jnp.float32
NY, NX, NH = 4, 4, 4
CHUNKS = 16
FIRST_Z = 10


def ladder_kernel(
    a_hbm, b_hbm, mine_ref, other_ref,
    a_v, b_v, c_v, r1_v, d_v, ra_v, rb_v, rc_v, rd_v, e_v, rz_v, m_v, o_v,
    a_sem, b_sem, ag_s, ag_r, s1_s, s1_r, sx_s, sx_r, sz_s, sz_r, so_s, so_r,
):
    nc, n1 = CHUNKS, FIRST_Z
    ch = b_v.shape[1]
    pair, virt = lax.axis_index("pair"), lax.axis_index("virt")
    y, z = pair // 2, pair % 2
    x, zh, core = virt // 8, (virt // 2) % 4, virt % 2

    def device(ny, nz, nx, nh, ncore):
        return {"pair": ny * 2 + nz, "virt": (nx * 4 + nh) * 2 + ncore}

    y_up, y_dn = (y + 1) % NY, (y + 3) % NY
    x_up, x_dn, x_far = (x + 1) % NX, (x + 3) % NX, (x + 2) % NX
    h_others = [(zh + 1) % NH, (zh + 3) % NH, (zh + 2) % NH]
    to_z = device(y, 1 - z, x, zh, core)
    to_up = device(y_up, z, x, zh, core)
    to_dn = device(y_dn, z, x, zh, core)
    to_core = device(y, z, x, zh, 1 - core)
    to_xu = device(y, z, x_up, zh, core)
    to_xd = device(y, z, x_dn, zh, core)
    to_xf = device(y, z, x_far, zh, core)
    to_h = [device(y, z, x, h, core) for h in h_others]
    partners = [to_z, to_up, to_dn, to_core, to_xu, to_xd, to_xf] + to_h

    b_copy = []
    for c in range(nc):
        cp = pltpu.make_async_copy(b_hbm.at[pl.ds(c * ch, ch)], b_v.at[z * nc + c], b_sem.at[c])
        cp.start()
        b_copy.append(cp)
    a_copy = []
    for c in range(nc):
        cp = pltpu.make_async_copy(a_hbm.at[:, pl.ds(c * ch, ch)], a_v.at[c], a_sem.at[c])
        cp.start()
        a_copy.append(cp)

    barrier = pltpu.get_barrier_semaphore()
    for dev in partners:
        pl.semaphore_signal(barrier, inc=1, device_id=dev, device_id_type=pl.DeviceIdType.MESH)
    pl.semaphore_wait(barrier, len(partners))

    def remote(src, dst, ssem, rsem, dev):
        return pltpu.make_async_remote_copy(
            src_ref=src, dst_ref=dst, send_sem=ssem, recv_sem=rsem,
            device_id=dev, device_id_type=pl.DeviceIdType.MESH,
        )

    def slot(s, rel, c):
        plane = z if rel == 0 else 1 - z
        return (s * 2 + plane) * nc + c

    def move(s_from, rel, s_to, rel_to, c, stream, dev):
        src = b_v.at[slot(s_from, rel, c)]
        dst = b_v.at[slot(s_to, rel, c)]
        remote(src, dst, ag_s.at[stream], ag_r.at[s_to * 2 + rel_to, c], dev).start()

    def send_z(s, c):
        move(s, 0, s, 1, c, 0, to_z)

    def send_up(rel, c):
        move(0, rel, 2, rel, c, 1, to_up)

    def send_dn(rel, c):
        move(0, rel, 1, rel, c, 2, to_dn)

    def relay_up(rel, c):
        move(2, rel, 3, rel, c, 1, to_up)

    def relay_dn(rel, c):
        move(1, rel, 3, rel, c, 2, to_dn)

    def arrived(s, rel, c):
        ref = b_v.at[slot(s, rel, c)]
        remote(ref, ref, ag_s.at[0], ag_r.at[s * 2 + rel, c], to_z).wait_recv()

    blocks = [(0, 0), (0, 1), (1, 0), (2, 0), (1, 1), (2, 1), (3, 0), (3, 1)]
    sets = [(0, 2), (2, 2), (4, 2), (6, 1), (7, 1)]

    def multiply(j, chunk0, count, first=False):
        u0, n = sets[j]
        starts = [slot(s, rel, 0) for s, rel in blocks[u0:u0 + n]]

        def body(i, _):
            k = chunk0 + 2 * i
            lhs = jnp.concatenate([a_v[k], a_v[k + 1]], axis=1)
            rhs = [jnp.concatenate([b_v[start + k], b_v[start + k + 1]], axis=0) for start in starts]
            rhs = jnp.concatenate(rhs, axis=1) if n == 2 else rhs[0]
            part = jnp.dot(lhs, rhs, preferred_element_type=F32)
            for t in range(n):
                piece = part[:, t * 128:(t + 1) * 128].reshape(16, 2, 32, 128)
                c_v[u0 + t] = piece if first else c_v[u0 + t] + piece
            return 0

        lax.fori_loop(0, count // 2, body, 0)

    def r_core(j):
        at = pl.ds(*sets[j])
        return remote(c_v.at[at, :, 1 - core], r1_v.at[at], s1_s.at[j], s1_r.at[j], to_core)

    def r_x(j, k):
        at = pl.ds(*sets[j])
        lo, hi = pl.ds(0, 2), pl.ds(2, 2)
        src, dst, dev = [
            (d_v.at[at, x_far, lo], ra_v.at[at], to_xu),
            (d_v.at[at, x_far, hi], rb_v.at[at], to_xd),
            (d_v.at[at, x_up, hi], rc_v.at[at, hi], to_xu),
            (d_v.at[at, x_dn, lo], rd_v.at[at, lo], to_xd),
            (d_v.at[at, x_up, lo], rc_v.at[at, lo], to_xu),
            (d_v.at[at, x_dn, hi], rd_v.at[at, hi], to_xd),
        ][k]
        return remote(src, dst, sx_s.at[j, k], sx_r.at[j, k], dev)

    def r_h(j, k):
        at = pl.ds(*sets[j])
        return remote(e_v.at[at, h_others[k]], rz_v.at[k, at], sz_s.at[j, k], sz_r.at[j, k], to_h[k])

    def r_far(j):
        at = pl.ds(*sets[j])
        return remote(m_v.at[at], o_v.at[at], so_s.at[j], so_r.at[j], to_xf)

    def stage1(j):
        r_core(j).start()

    def stage2(j):
        r_core(j).wait_recv()
        at = pl.ds(*sets[j])
        for k, xx in enumerate((x_far, x_up, x_dn, x)):
            rows = pl.ds(xx * NH, NH)
            d_v[at, xx] = c_v[at, rows, core] + r1_v[at, rows]
            if k == 0:
                r_x(j, 0).start()
                r_x(j, 1).start()
            if k == 1:
                r_x(j, 2).start()
            if k == 2:
                r_x(j, 3).start()

    def stage3(j):
        at = pl.ds(*sets[j])
        lo, hi = pl.ds(0, 2), pl.ds(2, 2)
        r_x(j, 0).wait_recv()
        d_v[at, x_up, lo] = d_v[at, x_up, lo] + ra_v[at]
        r_x(j, 4).start()
        r_x(j, 1).wait_recv()
        d_v[at, x_dn, hi] = d_v[at, x_dn, hi] + rb_v[at]
        r_x(j, 5).start()

    def stage4(j):
        at = pl.ds(*sets[j])
        for k in range(2, 6):
            r_x(j, k).wait_recv()
        e_v[at] = d_v[at, x] + rc_v[at] + rd_v[at]
        for k in (2, 0, 1):
            r_h(j, k).start()

    def stage5(j):
        at = pl.ds(*sets[j])
        for k in range(3):
            r_h(j, k).wait_recv()
        m_v[at] = e_v[at, zh] + rz_v[0, at] + rz_v[1, at] + rz_v[2, at]
        r_far(j).start()

    def stage6(j):
        r_far(j).wait_recv()
        u0, n = sets[j]
        for u in range(u0, u0 + n):
            s, rel = blocks[u]
            owner = [y, y_up, y_dn, (y + 2) % NY][s] * 2 + (z if rel == 0 else 1 - z)
            cols = pl.ds(pl.multiple_of(owner * 128, 128), 128)
            mine_ref[:, cols] = m_v[u]
            other_ref[:, cols] = o_v[u]

    for c in range(nc):
        b_copy[c].wait()
    for k in range(nc):
        send_z(0, k)
        late = (k + n1) % nc
        send_up(0, late)
        send_dn(0, late)
    for c in range(nc):
        a_copy[c].wait()

    late_pairs = (nc - n1) // 2
    for u in range(n1 // 2):
        lo, hi = 2 * u, 2 * u + 1
        if u < late_pairs:
            for c in (n1 + lo, n1 + hi):
                arrived(1, 0, c)
                arrived(2, 0, c)
            relay_up(0, n1 + lo)
            relay_dn(0, n1 + hi)
            for c in (n1 + lo, n1 + hi):
                send_z(1, c)
                send_z(2, c)
        for c in (lo, hi):
            arrived(0, 1, c)
            send_up(1, c)
            send_dn(1, c)
        if u == 0:
            multiply(0, 0, 2, True)
            multiply(1, n1, 2, True)
        else:
            multiply(0, lo, 2)
            if u < late_pairs:
                multiply(1, n1 + lo, 2)

    for u in range(n1 // 2):
        lo, hi = 2 * u, 2 * u + 1
        for c in (lo, hi):
            arrived(1, 0, c)
            arrived(2, 0, c)
        relay_up(0, lo)
        relay_dn(0, hi)
        multiply(1, lo, 2)
        if u >= n1 // 2 - late_pairs:
            c = n1 + 2 * (u - n1 // 2 + late_pairs)
            arrived(0, 1, c)
            arrived(0, 1, c + 1)
            multiply(0, c, 2)
    stage1(0)
    stage1(1)

    for u in range(n1 // 2):
        lo, hi = 2 * u, 2 * u + 1
        if u < late_pairs:
            for c in (n1 + lo, n1 + hi):
                arrived(3, 0, c)
                send_z(3, c)
        for c in (lo, hi):
            arrived(1, 1, c)
            arrived(2, 1, c)
        relay_up(1, lo)
        relay_dn(1, hi)
        if u == 0:
            multiply(2, 0, 2, True)
            multiply(3, n1, 2, True)
        else:
            multiply(2, lo, 2)
            if u < late_pairs:
                multiply(3, n1 + lo, 2)
        if u < 3:
            stage = [stage2, stage3, stage4][u]
            stage(0)
            stage(1)
    for c in range(n1, nc):
        arrived(1, 1, c)
        arrived(2, 1, c)
    multiply(2, n1, nc - n1)
    stage1(2)

    for u in range(n1 // 2):
        lo, hi = 2 * u, 2 * u + 1
        arrived(3, 0, lo)
        arrived(3, 0, hi)
        multiply(3, lo, 2)
        if u == 2:
            stage2(2)
    stage1(3)
    for c in range(n1, nc):
        arrived(3, 1, c)
    multiply(4, n1, 2, True)
    multiply(4, n1 + 2, nc - n1 - 2)
    stage5(0)
    stage5(1)

    for u in range(n1 // 2):
        lo, hi = 2 * u, 2 * u + 1
        arrived(3, 1, lo)
        arrived(3, 1, hi)
        multiply(4, lo, 2)
        if u == 0:
            stage2(3)
        if u == 1:
            stage3(2)
        if u == 2:
            stage6(0)
            stage6(1)
        if u == 3:
            stage3(3)
    stage1(4)
    stage4(2)
    stage4(3)
    stage2(4)
    stage5(2)
    stage3(4)
    stage5(3)
    stage4(4)
    stage6(2)
    stage6(3)
    stage5(4)
    stage6(4)

    relays = (nc + n1) // 2
    for stream, count in ((0, nc + 3 * (nc - n1)), (1, nc + n1 + relays), (2, nc + n1 + relays)):
        ref = b_v.at[pl.ds(0, count)]
        remote(ref, ref, ag_s.at[stream], ag_r.at[0, 0], to_z).wait_send()
    for j in range(len(sets)):
        for cp in [r_core(j), r_far(j)] + [r_x(j, k) for k in range(6)] + [r_h(j, k) for k in range(3)]:
            cp.wait_send()


def ladder_rows(amplitudes, integrals):
    rows, depth = amplitudes.shape
    ch = depth // CHUNKS
    vmem, dma = pltpu.VMEM, pltpu.SemaphoreType.DMA
    out = jax.ShapeDtypeStruct((32, 1024), F32)
    return pl.pallas_call(
        ladder_kernel,
        out_shape=(out, out),
        in_specs=[pl.BlockSpec(memory_space=pl.ANY)] * 2,
        out_specs=(pl.BlockSpec(memory_space=pltpu.VMEM),) * 2,
        scratch_shapes=[
            vmem((CHUNKS, rows, ch), jnp.bfloat16),
            vmem((8 * CHUNKS, ch, 128), jnp.bfloat16),
            vmem((8, 16, 2, 32, 128), F32),
            vmem((8, 16, 32, 128), F32),
            vmem((8, NX, NH, 32, 128), F32),
            vmem((8, 2, 32, 128), F32),
            vmem((8, 2, 32, 128), F32),
            vmem((8, NH, 32, 128), F32),
            vmem((8, NH, 32, 128), F32),
            vmem((8, NH, 32, 128), F32),
            vmem((3, 8, 32, 128), F32),
            vmem((8, 32, 128), F32),
            vmem((8, 32, 128), F32),
            dma((CHUNKS,)),
            dma((CHUNKS,)),
            dma((3,)),
            dma((8, CHUNKS)),
            dma((5,)),
            dma((5,)),
            dma((5, 6)),
            dma((5, 6)),
            dma((5, 3)),
            dma((5, 3)),
            dma((5,)),
            dma((5,)),
        ],
        compiler_params=pltpu.CompilerParams(collective_id=0, has_side_effects=True, vmem_limit_bytes=48 << 20),
    )(amplitudes, integrals)


def transpose_block(values, width):
    count = values.shape[0]
    return values.reshape(count, width, width).transpose(0, 2, 1).reshape(count, width * width)


def per_device(amplitudes, integrals, occ_pairs, partners, virt_list, eps_occ, eps_virt):
    width = virt_list.shape[0]
    mine, other = ladder_rows(amplitudes, integrals)
    flipped = jnp.take(other, partners % mine.shape[0], axis=0)
    total = mine + transpose_block(flipped, width)
    occ_ids = jnp.arange(eps_occ.shape[0], dtype=jnp.int32)
    occ_match = occ_pairs[:, :, None] == occ_ids[None, None, :]
    occ_sum = jnp.sum(jnp.where(occ_match, eps_occ[None, None, :], 0.0), axis=(1, 2))
    virt_ids = jnp.arange(eps_virt.shape[0], dtype=jnp.int32)
    virt_match = virt_list[:, None] == virt_ids[None, :]
    virt_energy = jnp.sum(jnp.where(virt_match, eps_virt[None, :], 0.0), axis=1)
    virt_sum = (virt_energy[:, None] + virt_energy[None, :]).reshape(-1)
    denominator = virt_sum[None, :] - occ_sum[:, None]
    return total / denominator


def solution(mesh):
    placed = (
        P("pair", "virt"),
        P("virt", "pair"),
        P(("pair", "virt"), None),
        P(("pair", "virt")),
        P(),
        P(),
        P(),
    )
    return jax.shard_map(
        per_device, mesh=mesh, in_specs=placed, out_specs=P(("pair", "virt"), None), check_vma=False
    )
```

time: 133 us -> 95.5 us (0.72); the launches traced: 131 us -> 95 us
  Pallas kernels: 127 us -> 91.1 us
    pallas_call x1, Pallas kernels: 127 us -> 91.1 us  [ladder_rows(): pl.pallas_call(ladder_kernel, out_shape=(out, out), in_specs=[pl.BlockSpe...]
where the time goes in v2:
time: 95.5 us; the launch traced here: 95 us
  Pallas kernels  91.1 us (95%)
  local copies, waits for them, and re-layouts  2.54 us (3%)
  other arithmetic  1.32 us (1%)
    pallas_call x1, Pallas kernels, ladder_rows(): pl.pallas_call(ladder_kernel, out_shape=(out, out), in_specs=[pl.BlockSpe...  91.1 us

profile of v2, /device:TPU:8, one launch (start us, length us, event | category | flops | bytes accessed | tf_op | source)
XLA Modules:
  0.0 95.0 jit_solution(8690406535967336306)
XLA Ops:
  0.0 0.0 copy-start
  0.0 1.2 %copy-done = bf16[4096,128]{1,0:T(8,128)(2,1)S(1)} copy-done((bf16[4096,128]{1,0:T(8,128)(2,1)S(1)}, bf16[4096,128]{1,0:T(8,128)(2,1)}, u32[]{:S(2)}) %copy-start) | copy-done | bytes 1048600
  1.2 0.0 copy-start.5
  1.2 0.0 copy-start.2
  1.2 0.0 copy-start.3
  1.2 0.0 copy-start.1
  1.2 0.0 copy-start.4
  1.2 91.1 %shard_map.73 = (f32[32,1024]{1,0:T(8,128)S(1)}, f32[32,1024]{1,0:T(8,128)S(1)}) custom-call(bf16[1024,4096]{1,0:T(8,128)(2,1)} %a_hbm.1, bf16[4096,128]{1,0:T(8,128)(2,1)S(1)} %copy-done), custom_call_target="tpu_custom_call" | custom-call | tf_op jit(solution)/shard_map/pallas_call | solution.py:322
  92.3 0.0 copy-done.5
  92.4 0.6 gather_fusion
  93.0 0.2 gather.7
  93.2 0.2 copy.10
  93.4 0.1 select_bitcast_fusion
  93.5 0.2 reshape.36
  93.7 0.0 copy-done.2
  93.8 0.0 copy-done.3
  93.8 0.2 select_reduce_fusion.1
  93.9 0.0 copy-done.1
  93.9 0.0 copy-done.4
  94.0 0.2 select_reduce_fusion
  94.1 0.1 broadcast_add_fusion
  94.2 0.1 add.41
  94.3 0.8 subtract_divide_fusion
  (2 shorter events, 0.0 us)
Async XLA Ops:
  0.0 1.2 %copy-start = (bf16[4096,128]{1,0:T(8,128)(2,1)S(1)}, bf16[4096,128]{1,0:T(8,128)(2,1)}, u32[]{:S(2)}) copy-start(bf16[4096,128]{1,0:T(8,128)(2,1)} %b_hbm.1) | copy-start | bytes 3145732
  1.2 91.1 %copy-start.5 = (s32[32]{0:T(128)S(1)}, s32[32]{0:T(128)}, u32[]{:S(2)}) copy-start(s32[32]{0:T(128)} %param.10) | copy-start | bytes 388
  1.2 92.5 %copy-start.2 = (s32[32,2]{0,1:T(2,128)S(1)}, s32[32,2]{0,1:T(2,128)}, u32[]{:S(2)}) copy-start(s32[32,2]{0,1:T(2,128)} %param.9) | copy-start | bytes 772
  1.2 92.5 %copy-start.3 = (f32[96]{0:T(128)S(1)}, f32[96]{0:T(128)}, u32[]{:S(2)}) copy-start(f32[96]{0:T(128)} %param.12) | copy-start | bytes 1156
  1.2 92.7 %copy-start.1 = (f32[512]{0:T(512)S(1)}, f32[512]{0:T(512)}, u32[]{:S(2)}) copy-start(f32[512]{0:T(512)} %param.13) | copy-start | bytes 6148
  1.2 92.7 %copy-start.4 = (s32[32]{0:T(128)S(1)}, s32[32]{0:T(128)}, u32[]{:S(2)}) copy-start(s32[32]{0:T(128)} %param.11) | copy-start | bytes 388

commit v3 on v2

--- a/solution.py
+++ b/solution.py
@@ -13,8 +13,9 @@
 
 def ladder_kernel(
     a_hbm, b_hbm, mine_ref, other_ref,
-    a_v, b_v, c_v, r1_v, d_v, ra_v, rb_v, rc_v, rd_v, e_v, rz_v, m_v, o_v,
+    a_v, b_v, c_v, r1_v, d_v, rf_v, rc_v, rd_v, e_v, rz_v, m_v, o_v,
     a_sem, b_sem, ag_s, ag_r, s1_s, s1_r, sx_s, sx_r, sz_s, sz_r, so_s, so_r,
+    z_known, x_known, h_known,
 ):
     nc, n1 = CHUNKS, FIRST_Z
     ch = b_v.shape[1]
@@ -36,23 +37,22 @@
     to_xd = device(y, z, x_dn, zh, core)
     to_xf = device(y, z, x_far, zh, core)
     to_h = [device(y, z, x, h, core) for h in h_others]
-    partners = [to_z, to_up, to_dn, to_core, to_xu, to_xd, to_xf] + to_h
-
+    to_zz = device(y, 1 - z, x, (zh + NH + 2 * z - 1) % NH, core)
+    near = [to_z, to_zz, to_up, to_dn, to_core, to_xu, to_xd]
+
+    barrier = pltpu.get_barrier_semaphore()
+
+    def signal(sem, dev):
+        pl.semaphore_signal(sem, inc=1, device_id=dev, device_id_type=pl.DeviceIdType.MESH)
+
+    for dev in near:
+        signal(barrier, dev)
     b_copy = []
     for c in range(nc):
         cp = pltpu.make_async_copy(b_hbm.at[pl.ds(c * ch, ch)], b_v.at[z * nc + c], b_sem.at[c])
         cp.start()
         b_copy.append(cp)
-    a_copy = []
-    for c in range(nc):
-        cp = pltpu.make_async_copy(a_hbm.at[:, pl.ds(c * ch, ch)], a_v.at[c], a_sem.at[c])
-        cp.start()
-        a_copy.append(cp)
-
-    barrier = pltpu.get_barrier_semaphore()
-    for dev in partners:
-        pl.semaphore_signal(barrier, inc=1, device_id=dev, device_id_type=pl.DeviceIdType.MESH)
-    pl.semaphore_wait(barrier, len(partners))
+    pl.semaphore_wait(barrier, len(near))
 
     def remote(src, dst, ssem, rsem, dev):
         return pltpu.make_async_remote_copy(
@@ -108,22 +108,16 @@
 
         lax.fori_loop(0, count // 2, body, 0)
 
-    def r_core(j):
-        at = pl.ds(*sets[j])
-        return remote(c_v.at[at, :, 1 - core], r1_v.at[at], s1_s.at[j], s1_r.at[j], to_core)
+    x_order = [x_far, x_up, x_dn, x]
+
+    def r_core(j, k):
+        at, rows = pl.ds(*sets[j]), pl.ds(x_order[k] * NH, NH)
+        return remote(c_v.at[at, rows, 1 - core], r1_v.at[at, rows], s1_s.at[j, k], s1_r.at[j, k], to_core)
 
     def r_x(j, k):
         at = pl.ds(*sets[j])
-        lo, hi = pl.ds(0, 2), pl.ds(2, 2)
-        src, dst, dev = [
-            (d_v.at[at, x_far, lo], ra_v.at[at], to_xu),
-            (d_v.at[at, x_far, hi], rb_v.at[at], to_xd),
-            (d_v.at[at, x_up, hi], rc_v.at[at, hi], to_xu),
-            (d_v.at[at, x_dn, lo], rd_v.at[at, lo], to_xd),
-            (d_v.at[at, x_up, lo], rc_v.at[at, lo], to_xu),
-            (d_v.at[at, x_dn, hi], rd_v.at[at, hi], to_xd),
-        ][k]
-        return remote(src, dst, sx_s.at[j, k], sx_r.at[j, k], dev)
+        dst, dev = [(rf_v, to_xf), (rc_v, to_xu), (rd_v, to_xd)][k]
+        return remote(d_v.at[at, x_order[k]], dst.at[at], sx_s.at[j, k], sx_r.at[j, k], dev)
 
     def r_h(j, k):
         at = pl.ds(*sets[j])
@@ -134,48 +128,34 @@
         return remote(m_v.at[at], o_v.at[at], so_s.at[j], so_r.at[j], to_xf)
 
     def stage1(j):
-        r_core(j).start()
+        for k in range(4):
+            r_core(j, k).start()
 
     def stage2(j):
-        r_core(j).wait_recv()
-        at = pl.ds(*sets[j])
-        for k, xx in enumerate((x_far, x_up, x_dn, x)):
+        at = pl.ds(*sets[j])
+        for k, xx in enumerate(x_order):
             rows = pl.ds(xx * NH, NH)
+            r_core(j, k).wait_recv()
             d_v[at, xx] = c_v[at, rows, core] + r1_v[at, rows]
-            if k == 0:
-                r_x(j, 0).start()
-                r_x(j, 1).start()
-            if k == 1:
-                r_x(j, 2).start()
-            if k == 2:
-                r_x(j, 3).start()
+            if k < 3:
+                r_x(j, k).start()
 
     def stage3(j):
         at = pl.ds(*sets[j])
-        lo, hi = pl.ds(0, 2), pl.ds(2, 2)
-        r_x(j, 0).wait_recv()
-        d_v[at, x_up, lo] = d_v[at, x_up, lo] + ra_v[at]
-        r_x(j, 4).start()
-        r_x(j, 1).wait_recv()
-        d_v[at, x_dn, hi] = d_v[at, x_dn, hi] + rb_v[at]
-        r_x(j, 5).start()
-
-    def stage4(j):
-        at = pl.ds(*sets[j])
-        for k in range(2, 6):
+        for k in range(3):
             r_x(j, k).wait_recv()
-        e_v[at] = d_v[at, x] + rc_v[at] + rd_v[at]
+        e_v[at] = d_v[at, x] + rc_v[at] + rd_v[at] + rf_v[at]
         for k in (2, 0, 1):
             r_h(j, k).start()
 
-    def stage5(j):
+    def stage4(j):
         at = pl.ds(*sets[j])
         for k in range(3):
             r_h(j, k).wait_recv()
         m_v[at] = e_v[at, zh] + rz_v[0, at] + rz_v[1, at] + rz_v[2, at]
         r_far(j).start()
 
-    def stage6(j):
+    def stage5(j):
         r_far(j).wait_recv()
         u0, n = sets[j]
         for u in range(u0, u0 + n):
@@ -192,8 +172,20 @@
         late = (k + n1) % nc
         send_up(0, late)
         send_dn(0, late)
+    signal(z_known, to_z)
+    signal(z_known, to_zz)
+    signal(x_known, to_xu)
+    signal(x_known, to_xd)
+    a_copy = []
+    for c in range(nc):
+        cp = pltpu.make_async_copy(a_hbm.at[:, pl.ds(c * ch, ch)], a_v.at[c], a_sem.at[c])
+        cp.start()
+        a_copy.append(cp)
     for c in range(nc):
         a_copy[c].wait()
+    pl.semaphore_wait(z_known, 2)
+    signal(h_known, to_h[0])
+    signal(h_known, to_h[1])
 
     late_pairs = (nc - n1) // 2
     for u in range(n1 // 2):
@@ -232,6 +224,8 @@
             arrived(0, 1, c)
             arrived(0, 1, c + 1)
             multiply(0, c, 2)
+    pl.semaphore_wait(x_known, 2)
+    pl.semaphore_wait(h_known, 2)
     stage1(0)
     stage1(1)
 
@@ -253,8 +247,8 @@
             multiply(2, lo, 2)
             if u < late_pairs:
                 multiply(3, n1 + lo, 2)
-        if u < 3:
-            stage = [stage2, stage3, stage4][u]
+        if u in (0, 3):
+            stage = stage2 if u == 0 else stage3
             stage(0)
             stage(1)
     for c in range(n1, nc):
@@ -275,8 +269,6 @@
         arrived(3, 1, c)
     multiply(4, n1, 2, True)
     multiply(4, n1 + 2, nc - n1 - 2)
-    stage5(0)
-    stage5(1)
 
     for u in range(n1 // 2):
         lo, hi = 2 * u, 2 * u + 1
@@ -285,32 +277,28 @@
         multiply(4, lo, 2)
         if u == 0:
             stage2(3)
-        if u == 1:
-            stage3(2)
-        if u == 2:
-            stage6(0)
-            stage6(1)
-        if u == 3:
-            stage3(3)
     stage1(4)
+    stage2(4)
+    stage3(2)
+    stage3(3)
+    stage3(4)
+    stage4(0)
+    stage4(1)
     stage4(2)
     stage4(3)
-    stage2(4)
+    stage4(4)
+    stage5(0)
+    stage5(1)
     stage5(2)
-    stage3(4)
     stage5(3)
-    stage4(4)
-    stage6(2)
-    stage6(3)
     stage5(4)
-    stage6(4)
 
     relays = (nc + n1) // 2
     for stream, count in ((0, nc + 3 * (nc - n1)), (1, nc + n1 + relays), (2, nc + n1 + relays)):
         ref = b_v.at[pl.ds(0, count)]
         remote(ref, ref, ag_s.at[stream], ag_r.at[0, 0], to_z).wait_send()
     for j in range(len(sets)):
-        for cp in [r_core(j), r_far(j)] + [r_x(j, k) for k in range(6)] + [r_h(j, k) for k in range(3)]:
+        for cp in [r_far(j)] + [r_core(j, k) for k in range(4)] + [r_x(j, k) for k in range(3)] + [r_h(j, k) for k in range(3)]:
             cp.wait_send()
 
 
@@ -330,8 +318,7 @@
             vmem((8, 16, 2, 32, 128), F32),
             vmem((8, 16, 32, 128), F32),
             vmem((8, NX, NH, 32, 128), F32),
-            vmem((8, 2, 32, 128), F32),
-            vmem((8, 2, 32, 128), F32),
+            vmem((8, NH, 32, 128), F32),
             vmem((8, NH, 32, 128), F32),
             vmem((8, NH, 32, 128), F32),
             vmem((8, NH, 32, 128), F32),
@@ -342,16 +329,19 @@
             dma((CHUNKS,)),
             dma((3,)),
             dma((8, CHUNKS)),
-            dma((5,)),
-            dma((5,)),
-            dma((5, 6)),
-            dma((5, 6)),
+            dma((5, 4)),
+            dma((5, 4)),
+            dma((5, 3)),
+            dma((5, 3)),
             dma((5, 3)),
             dma((5, 3)),
             dma((5,)),
             dma((5,)),
+            pltpu.SemaphoreType.REGULAR,
+            pltpu.SemaphoreType.REGULAR,
+            pltpu.SemaphoreType.REGULAR,
         ],
-        compiler_params=pltpu.CompilerParams(collective_id=0, has_side_effects=True, vmem_limit_bytes=48 << 20),
+        compiler_params=pltpu.CompilerParams(collective_id=0, has_side_effects=True, vmem_limit_bytes=63 << 20),
     )(amplitudes, integrals)
 
 

time: 95.5 us -> 87.7 us (0.918)
  Pallas kernels: 91.1 us -> 81.8 us
    pallas_call x1, Pallas kernels: 91.1 us -> 81.8 us  [ladder_rows(): pl.pallas_call(ladder_kernel, out_shape=(out, out), in_specs=[pl.BlockSpe...]
    unnamed x12 -> x10, local copies, waits for them, and re-layouts: 1.24 us -> 0.02 us
    gather x3, local copies, waits for them, and re-layouts: 0.98 us -> 1.94 us  [per_device(): flipped = jnp.take(other, partners % mine.shape[0], axis=0)]
where the time goes in v3:
time: 87.7 us; the launch traced here: 86.4 us
  Pallas kernels  81.8 us (93%)
  local copies, waits for them, and re-layouts  2.27 us (3%)
  other arithmetic  2.22 us (3%)
    pallas_call x1, Pallas kernels, ladder_rows(): pl.pallas_call(ladder_kernel, out_shape=(out, out), in_specs=[pl.BlockSpe...  81.8 us
    gather x3, local copies, waits for them, and re-layouts, per_device(): flipped = jnp.take(other, partners % mine.shape[0], axis=0)  1.94 us

profile of v3, /device:TPU:8, one launch (start us, length us, event | category | flops | bytes accessed | tf_op | source)
XLA Modules:
  0.0 86.4 jit_solution(3215954084000012565)
XLA Ops:
  0.0 0.0 copy-start.4
  0.0 0.0 copy-start.2
  0.0 0.0 copy-start.1
  0.0 0.0 copy-start
  0.0 0.0 copy-start.3
  0.0 81.8 %shard_map.73 = (f32[32,1024]{1,0:T(8,128)}, f32[32,1024]{1,0:T(8,128)}) custom-call(bf16[1024,4096]{1,0:T(8,128)(2,1)} %a_hbm.1, bf16[4096,128]{1,0:T(8,128)(2,1)} %b_hbm.1), custom_call_target="tpu_custom_call" | custom-call | tf_op jit(solution)/shard_map/pallas_call | solution.py:310
  81.9 0.0 copy-done.4
  81.9 1.6 %gather_fusion = f32[32,1024]{1,0:T(8,128)S(1)} fusion(f32[32,1024]{1,0:T(8,128)} %get-tuple-element.8, s32[1024]{0:T(1024)S(1)} %pad_clamp_fusion), kind=kCustom, calls=%fused_computation | custom fusion | bytes 262272 | tf_op jit(solution)/shard_map/jit(_take)/gather | solution.py:356
  83.5 0.2 gather.7
  83.7 0.2 copy.10
  83.9 0.1 select_bitcast_fusion
  84.0 0.2 reshape.36
  84.2 0.0 copy-done.2
  84.2 0.0 copy-done.1
  84.2 0.2 select_reduce_fusion.1
  84.4 0.0 copy-done
  84.4 0.0 copy-done.3
  84.4 0.2 select_reduce_fusion
  84.6 0.1 broadcast_add_fusion
  84.7 0.1 add.41
  84.8 1.7 %subtract_divide_fusion = f32[32,1024]{1,0:T(8,128)} fusion(f32[32,1024]{1,0:T(8,128)} %get-tuple-element.7, f32[32,1024]{1,0:T(8,128)S(1)} %reshape.36, f32[32]{0:T(128)S(1)} %select_reduce_fusion.1, f32[1024]{0:T(1024)S(1)} %add.41), kind=kLoop, calls=%fused_computation.2 | loop fusion | flops 98304 | bytes 397440 | tf_op jit(solution)/shard_map/div | solution.py:366
  (2 shorter events, 0.0 us)
Async XLA Ops:
  0.0 81.9 %copy-start.4 = (s32[32]{0:T(128)S(1)}, s32[32]{0:T(128)}, u32[]{:S(2)}) copy-start(s32[32]{0:T(128)} %param.10) | copy-start | bytes 388
  0.0 84.2 %copy-start.2 = (f32[96]{0:T(128)S(1)}, f32[96]{0:T(128)}, u32[]{:S(2)}) copy-start(f32[96]{0:T(128)} %param.12) | copy-start | bytes 1156
  0.0 84.2 %copy-start.1 = (s32[32,2]{0,1:T(2,128)S(1)}, s32[32,2]{0,1:T(2,128)}, u32[]{:S(2)}) copy-start(s32[32,2]{0,1:T(2,128)} %param.9) | copy-start | bytes 772
  0.0 84.4 %copy-start = (f32[512]{0:T(512)S(1)}, f32[512]{0:T(512)}, u32[]{:S(2)}) copy-start(f32[512]{0:T(512)} %param.13) | copy-start | bytes 6148
  0.0 84.4 %copy-start.3 = (s32[32]{0:T(128)S(1)}, s32[32]{0:T(128)}, u32[]{:S(2)}) copy-start(s32[32]{0:T(128)} %param.11) | copy-start | bytes 388

commit v4 on v3

--- a/solution.py
+++ b/solution.py
@@ -9,11 +9,13 @@
 NY, NX, NH = 4, 4, 4
 CHUNKS = 16
 FIRST_Z = 10
+TOP = 32767.0
+LIFT = 2.0 ** 60
 
 
 def ladder_kernel(
     a_hbm, b_hbm, mine_ref, other_ref,
-    a_v, b_v, c_v, r1_v, d_v, rf_v, rc_v, rd_v, e_v, rz_v, m_v, o_v,
+    a_v, b_v, c_v, r1_v, d_v, dq_v, ds_v, rq_v, rs_v, e_v, eq_v, es_v, rzq_v, rzs_v, m_v, o_v,
     a_sem, b_sem, ag_s, ag_r, s1_s, s1_r, sx_s, sx_r, sz_s, sz_r, so_s, so_r,
     z_known, x_known, h_known,
 ):
@@ -114,14 +116,28 @@
         at, rows = pl.ds(*sets[j]), pl.ds(x_order[k] * NH, NH)
         return remote(c_v.at[at, rows, 1 - core], r1_v.at[at, rows], s1_s.at[j, k], s1_r.at[j, k], to_core)
 
+    def coded(value):
+        most = jnp.max(jnp.abs(value), axis=2, keepdims=True)
+        inverse = jnp.where(most > 0.0, TOP / jnp.maximum(most * LIFT, 1e-20), 0.0)
+        level = jnp.floor((value * LIFT) * inverse + 0.5)
+        return level.astype(jnp.int32).astype(jnp.int16), most * (1.0 / TOP)
+
+    def decoded(level, scale):
+        return level.astype(jnp.int32).astype(F32) * scale
+
     def r_x(j, k):
-        at = pl.ds(*sets[j])
-        dst, dev = [(rf_v, to_xf), (rc_v, to_xu), (rd_v, to_xd)][k]
-        return remote(d_v.at[at, x_order[k]], dst.at[at], sx_s.at[j, k], sx_r.at[j, k], dev)
+        at, dev = pl.ds(*sets[j]), [to_xf, to_xu, to_xd][k]
+        return [
+            remote(dq_v.at[k, at], rq_v.at[k, at], sx_s.at[j, k], sx_r.at[j, k], dev),
+            remote(ds_v.at[k, at], rs_v.at[k, at], sx_s.at[j, 3 + k], sx_r.at[j, 3 + k], dev),
+        ]
 
     def r_h(j, k):
         at = pl.ds(*sets[j])
-        return remote(e_v.at[at, h_others[k]], rz_v.at[k, at], sz_s.at[j, k], sz_r.at[j, k], to_h[k])
+        return [
+            remote(eq_v.at[at, h_others[k]], rzq_v.at[k, at], sz_s.at[j, k], sz_r.at[j, k], to_h[k]),
+            remote(es_v.at[at, h_others[k]], rzs_v.at[k, at], sz_s.at[j, 3 + k], sz_r.at[j, 3 + k], to_h[k]),
+        ]
 
     def r_far(j):
         at = pl.ds(*sets[j])
@@ -136,23 +152,35 @@
         for k, xx in enumerate(x_order):
             rows = pl.ds(xx * NH, NH)
             r_core(j, k).wait_recv()
-            d_v[at, xx] = c_v[at, rows, core] + r1_v[at, rows]
-            if k < 3:
-                r_x(j, k).start()
+            total = c_v[at, rows, core] + r1_v[at, rows]
+            if k == 3:
+                d_v[at] = total
+            else:
+                dq_v[k, at], ds_v[k, at] = coded(total)
+                for cp in r_x(j, k):
+                    cp.start()
 
     def stage3(j):
         at = pl.ds(*sets[j])
-        for k in range(3):
-            r_x(j, k).wait_recv()
-        e_v[at] = d_v[at, x] + rc_v[at] + rd_v[at] + rf_v[at]
+        total = d_v[at]
+        for k in (1, 2, 0):
+            for cp in r_x(j, k):
+                cp.wait_recv()
+            total = total + decoded(rq_v[k, at], rs_v[k, at])
+        e_v[at] = total
+        eq_v[at], es_v[at] = coded(total)
         for k in (2, 0, 1):
-            r_h(j, k).start()
+            for cp in r_h(j, k):
+                cp.start()
 
     def stage4(j):
         at = pl.ds(*sets[j])
+        total = e_v[at, zh]
         for k in range(3):
-            r_h(j, k).wait_recv()
-        m_v[at] = e_v[at, zh] + rz_v[0, at] + rz_v[1, at] + rz_v[2, at]
+            for cp in r_h(j, k):
+                cp.wait_recv()
+            total = total + decoded(rzq_v[k, at], rzs_v[k, at])
+        m_v[at] = total
         r_far(j).start()
 
     def stage5(j):
@@ -298,8 +326,12 @@
         ref = b_v.at[pl.ds(0, count)]
         remote(ref, ref, ag_s.at[stream], ag_r.at[0, 0], to_z).wait_send()
     for j in range(len(sets)):
-        for cp in [r_far(j)] + [r_core(j, k) for k in range(4)] + [r_x(j, k) for k in range(3)] + [r_h(j, k) for k in range(3)]:
-            cp.wait_send()
+        r_far(j).wait_send()
+        for k in range(4):
+            r_core(j, k).wait_send()
+        for k in range(3):
+            for cp in r_x(j, k) + r_h(j, k):
+                cp.wait_send()
 
 
 def ladder_rows(amplitudes, integrals):
@@ -317,12 +349,16 @@
             vmem((8 * CHUNKS, ch, 128), jnp.bfloat16),
             vmem((8, 16, 2, 32, 128), F32),
             vmem((8, 16, 32, 128), F32),
-            vmem((8, NX, NH, 32, 128), F32),
             vmem((8, NH, 32, 128), F32),
+            vmem((3, 8, NH, 32, 128), jnp.int16),
+            vmem((3, 8, NH, 1, 128), F32),
+            vmem((3, 8, NH, 32, 128), jnp.int16),
+            vmem((3, 8, NH, 1, 128), F32),
             vmem((8, NH, 32, 128), F32),
-            vmem((8, NH, 32, 128), F32),
-            vmem((8, NH, 32, 128), F32),
-            vmem((3, 8, 32, 128), F32),
+            vmem((8, NH, 32, 128), jnp.int16),
+            vmem((8, NH, 1, 128), F32),
+            vmem((3, 8, 32, 128), jnp.int16),
+            vmem((3, 8, 1, 128), F32),
             vmem((8, 32, 128), F32),
             vmem((8, 32, 128), F32),
             dma((CHUNKS,)),
@@ -331,10 +367,10 @@
             dma((8, CHUNKS)),
             dma((5, 4)),
             dma((5, 4)),
-            dma((5, 3)),
-            dma((5, 3)),
-            dma((5, 3)),
-            dma((5, 3)),
+            dma((5, 6)),
+            dma((5, 6)),
+            dma((5, 6)),
+            dma((5, 6)),
             dma((5,)),
             dma((5,)),
             pltpu.SemaphoreType.REGULAR,

time: 87.7 us -> 86.8 us (0.990)
  Pallas kernels: 81.8 us -> 80.9 us
    pallas_call x1, Pallas kernels: 81.8 us -> 80.9 us  [ladder_rows(): pl.pallas_call(ladder_kernel, out_shape=(out, out), in_specs=[pl.BlockSpe...]
where the time goes in v4:
time: 86.8 us; the launch traced here: 85.5 us
  Pallas kernels  80.9 us (93%)
  local copies, waits for them, and re-layouts  2.27 us (3%)
  other arithmetic  2.22 us (3%)
    pallas_call x1, Pallas kernels, ladder_rows(): pl.pallas_call(ladder_kernel, out_shape=(out, out), in_specs=[pl.BlockSpe...  80.9 us
    gather x3, local copies, waits for them, and re-layouts, per_device(): flipped = jnp.take(other, partners % mine.shape[0], axis=0)  1.94 us

profile of v4, /device:TPU:8, one launch (start us, length us, event | category | flops | bytes accessed | tf_op | source)
XLA Modules:
  0.0 85.5 jit_solution(13426888328278247649)
XLA Ops:
  0.0 0.0 copy-start.4
  0.0 0.0 copy-start.2
  0.0 0.0 copy-start.1
  0.0 0.0 copy-start
  0.0 0.0 copy-start.3
  0.0 80.9 %shard_map.73 = (f32[32,1024]{1,0:T(8,128)}, f32[32,1024]{1,0:T(8,128)}) custom-call(bf16[1024,4096]{1,0:T(8,128)(2,1)} %a_hbm.1, bf16[4096,128]{1,0:T(8,128)(2,1)} %b_hbm.1), custom_call_target="tpu_custom_call" | custom-call | tf_op jit(solution)/shard_map/pallas_call | solution.py:342
  81.0 0.0 copy-done.4
  81.0 1.6 %gather_fusion = f32[32,1024]{1,0:T(8,128)S(1)} fusion(f32[32,1024]{1,0:T(8,128)} %get-tuple-element.8, s32[1024]{0:T(1024)S(1)} %pad_clamp_fusion), kind=kCustom, calls=%fused_computation | custom fusion | bytes 262272 | tf_op jit(solution)/shard_map/jit(_take)/gather | solution.py:392
  82.6 0.2 gather.7
  82.8 0.2 copy.10
  83.0 0.1 select_bitcast_fusion
  83.1 0.2 reshape.36
  83.3 0.0 copy-done.2
  83.3 0.0 copy-done.1
  83.3 0.2 select_reduce_fusion.1
  83.5 0.0 copy-done
  83.5 0.0 copy-done.3
  83.5 0.2 select_reduce_fusion
  83.7 0.1 broadcast_add_fusion
  83.8 0.1 add.41
  83.9 1.7 %subtract_divide_fusion = f32[32,1024]{1,0:T(8,128)} fusion(f32[32,1024]{1,0:T(8,128)} %get-tuple-element.7, f32[32,1024]{1,0:T(8,128)S(1)} %reshape.36, f32[32]{0:T(128)S(1)} %select_reduce_fusion.1, f32[1024]{0:T(1024)S(1)} %add.41), kind=kLoop, calls=%fused_computation.2 | loop fusion | flops 98304 | bytes 397440 | tf_op jit(solution)/shard_map/div | solution.py:402
  (2 shorter events, 0.0 us)
Async XLA Ops:
  0.0 81.0 %copy-start.4 = (s32[32]{0:T(128)S(1)}, s32[32]{0:T(128)}, u32[]{:S(2)}) copy-start(s32[32]{0:T(128)} %param.10) | copy-start | bytes 388
  0.0 83.3 %copy-start.2 = (f32[96]{0:T(128)S(1)}, f32[96]{0:T(128)}, u32[]{:S(2)}) copy-start(f32[96]{0:T(128)} %param.12) | copy-start | bytes 1156
  0.0 83.3 %copy-start.1 = (s32[32,2]{0,1:T(2,128)S(1)}, s32[32,2]{0,1:T(2,128)}, u32[]{:S(2)}) copy-start(s32[32,2]{0,1:T(2,128)} %param.9) | copy-start | bytes 772
  0.0 83.5 %copy-start = (f32[512]{0:T(512)S(1)}, f32[512]{0:T(512)}, u32[]{:S(2)}) copy-start(f32[512]{0:T(512)} %param.13) | copy-start | bytes 6148
  0.0 83.5 %copy-start.3 = (s32[32]{0:T(128)S(1)}, s32[32]{0:T(128)}, u32[]{:S(2)}) copy-start(s32[32]{0:T(128)} %param.11) | copy-start | bytes 388

commit v5 on v4

--- a/solution.py
+++ b/solution.py
@@ -168,8 +168,9 @@
                 cp.wait_recv()
             total = total + decoded(rq_v[k, at], rs_v[k, at])
         e_v[at] = total
-        eq_v[at], es_v[at] = coded(total)
         for k in (2, 0, 1):
+            piece = pl.ds(h_others[k], 1)
+            eq_v[at, piece], es_v[at, piece] = coded(e_v[at, piece])
             for cp in r_h(j, k):
                 cp.start()
 
@@ -319,8 +320,6 @@
     stage5(1)
     stage5(2)
     stage5(3)
-    stage5(4)
-
     relays = (nc + n1) // 2
     for stream, count in ((0, nc + 3 * (nc - n1)), (1, nc + n1 + relays), (2, nc + n1 + relays)):
         ref = b_v.at[pl.ds(0, count)]
@@ -332,6 +331,8 @@
         for k in range(3):
             for cp in r_x(j, k) + r_h(j, k):
                 cp.wait_send()
+
+    stage5(4)
 
 
 def ladder_rows(amplitudes, integrals):
@@ -389,7 +390,7 @@
 def per_device(amplitudes, integrals, occ_pairs, partners, virt_list, eps_occ, eps_virt):
     width = virt_list.shape[0]
     mine, other = ladder_rows(amplitudes, integrals)
-    flipped = jnp.take(other, partners % mine.shape[0], axis=0)
+    flipped = jnp.take(other, partners % mine.shape[0], axis=0, mode="clip")
     total = mine + transpose_block(flipped, width)
     occ_ids = jnp.arange(eps_occ.shape[0], dtype=jnp.int32)
     occ_match = occ_pairs[:, :, None] == occ_ids[None, None, :]

time: 86.8 us -> 86.6 us (level)
    gather x3 -> x1, local copies, waits for them, and re-layouts: 1.94 us -> 1.58 us  [per_device(): flipped = jnp.take(other, partners % mine.shape[0], axis=0, mode='clip')]
where the time goes in v5:
time: 86.6 us; the launch traced here: 85.3 us
  Pallas kernels  80.8 us (93%)
  local copies, waits for them, and re-layouts  2.27 us (3%)
  other arithmetic  2.11 us (2%)
    pallas_call x1, Pallas kernels, ladder_rows(): pl.pallas_call(ladder_kernel, out_shape=(out, out), in_specs=[pl.BlockSpe...  80.8 us

profile of v5, /device:TPU:8, one launch (start us, length us, event | category | flops | bytes accessed | tf_op | source)
XLA Modules:
  0.0 85.3 jit_solution(3846034291334528912)
XLA Ops:
  0.0 0.0 copy-start.4
  0.0 0.0 copy-start.2
  0.0 0.0 copy-start.1
  0.0 0.0 copy-start
  0.0 0.0 copy-start.3
  0.0 80.8 %shard_map.73 = (f32[32,1024]{1,0:T(8,128)}, f32[32,1024]{1,0:T(8,128)}) custom-call(bf16[1024,4096]{1,0:T(8,128)(2,1)} %a_hbm.1, bf16[4096,128]{1,0:T(8,128)(2,1)} %b_hbm.1), custom_call_target="tpu_custom_call" | custom-call | tf_op jit(solution)/shard_map/pallas_call | solution.py:343
  80.8 0.0 copy-done.4
  80.9 1.6 %gather_fusion = f32[32,1024]{1,0:T(8,128)S(1)} fusion(f32[32,1024]{1,0:T(8,128)} %get-tuple-element.8, s32[1024]{0:T(1024)S(1)} %pad_clamp_fusion), kind=kCustom, calls=%fused_computation | custom fusion | bytes 262272 | tf_op jit(solution)/shard_map/jit(_take)/gather | solution.py:393
  82.4 0.2 reshape.27
  82.6 0.2 copy.10
  82.8 0.2 reshape.28
  83.1 0.0 copy-done.2
  83.1 0.0 copy-done.1
  83.1 0.2 select_reduce_fusion.1
  83.3 0.0 copy-done
  83.3 0.0 copy-done.3
  83.3 0.2 select_reduce_fusion
  83.5 0.1 broadcast_add_fusion
  83.5 0.1 add.34
  83.6 1.7 %subtract_divide_fusion = f32[32,1024]{1,0:T(8,128)} fusion(f32[32,1024]{1,0:T(8,128)} %get-tuple-element.7, f32[32,1024]{1,0:T(8,128)S(1)} %reshape.28, f32[32]{0:T(128)S(1)} %select_reduce_fusion.1, f32[1024]{0:T(1024)S(1)} %add.34), kind=kLoop, calls=%fused_computation.1 | loop fusion | flops 98304 | bytes 397440 | tf_op jit(solution)/shard_map/div | solution.py:403
  (2 shorter events, 0.0 us)
Async XLA Ops:
  0.0 80.8 %copy-start.4 = (s32[32]{0:T(128)S(1)}, s32[32]{0:T(128)}, u32[]{:S(2)}) copy-start(s32[32]{0:T(128)} %param.10) | copy-start | bytes 388
  0.0 83.1 %copy-start.2 = (f32[96]{0:T(128)S(1)}, f32[96]{0:T(128)}, u32[]{:S(2)}) copy-start(f32[96]{0:T(128)} %param.12) | copy-start | bytes 1156
  0.0 83.1 %copy-start.1 = (s32[32,2]{0,1:T(2,128)S(1)}, s32[32,2]{0,1:T(2,128)}, u32[]{:S(2)}) copy-start(s32[32,2]{0,1:T(2,128)} %param.9) | copy-start | bytes 772
  0.0 83.3 %copy-start = (f32[512]{0:T(512)S(1)}, f32[512]{0:T(512)}, u32[]{:S(2)}) copy-start(f32[512]{0:T(512)} %param.13) | copy-start | bytes 6148
  0.0 83.3 %copy-start.3 = (s32[32]{0:T(128)S(1)}, s32[32]{0:T(128)}, u32[]{:S(2)}) copy-start(s32[32]{0:T(128)} %param.11) | copy-start | bytes 388
